TPU v7x, 32 devices: a whole 2x2x4 slice. The times are simulated.
32 devices in a mesh: band: 16 (over z, y, core), helper: 2 (over x).
Axes of the slice: x: 2, y: 2, z: 4, core: 2. Of those that a mesh axis runs over, the one named last changes fastest.
Arguments:
- node_latent: bfloat16 [2048, 256], P(('band', 'helper')), may hold values from -6 to 6
- edge_latent: bfloat16 [32768, 256], P(('band', 'helper')), may hold values from -6 to 6
- grad_out_node: bfloat16 [2048, 256], P(('band', 'helper')), may hold values from -6 to 6
- grad_out_edge: bfloat16 [32768, 256], P(('band', 'helper')), may hold values from -6 to 6
- senders: int32 [32768], P(('band', 'helper')), may hold values from 0 to 191
- receivers: int32 [32768], P(('band', 'helper')), may hold values from 0 to 127, as said below
- band_edges: int32 [16], replicated, may hold values from 2 to 16, as said below
- halo_list: int32 [16, 32], P('band'), may hold values from 0 to 127, as said below
- sea_mask: int32 [2048], P(('band', 'helper')), may hold values 0 or 1
- edge_w1: bfloat16 [768, 256], replicated, may hold values from -0.21875 to 0.21875
- edge_b1: float32 [256], replicated, may hold values from -3 to 3
- edge_w2: bfloat16 [256, 256], replicated, may hold values from -0.375 to 0.375
- edge_b2: float32 [256], replicated, may hold values from -3 to 3
- node_w1: bfloat16 [512, 256], replicated, may hold values from -0.25 to 0.25
- node_b1: float32 [256], replicated, may hold values from -3 to 3
- node_w2: bfloat16 [256, 256], replicated, may hold values from -0.375 to 0.375
- node_b2: float32 [256], replicated, may hold values from -3 to 3
Outputs:
- grad_node: float32 [2048, 256], P(('band', 'helper'))
- grad_edge: bfloat16 [32768, 256], P(('band', 'helper'))
- grad_edge_w1: float32 [768, 256], replicated
- grad_edge_b1: float32 [256], replicated
- grad_edge_w2: float32 [256, 256], replicated
- grad_edge_b2: float32 [256], replicated
- grad_node_w1: float32 [512, 256], replicated
- grad_node_b1: float32 [256], replicated
- grad_node_w2: float32 [256, 256], replicated
- grad_node_b2: float32 [256], replicated
Inputs may be any that keep to these rules, and one draw needn't show every extreme that they name: In every aligned block of 128 edge rows, all receivers lie in one aligned tile of 64 nodes. `band_edges`: A quarter of the bands, consecutive along the cycle, hold 16 live blocks; every other band holds between 2 and 6. `halo_list`: the 32 entries of a band are distinct.
All inputs are finite; a program needn't handle non-finite values. No bound on the sum of `sea_mask` on one device may be relied on, other than what follows from the above.
Results may differ from a plain program's by a relative error of at most 0.01.
Values may be sent and summed in bfloat16 or wider, within the bound.
No kernel may reach another device: no remote copies, remote signals or barrier semaphores. Data moves between devices by JAX's collectives and lax.ppermute only.
A program may use at most 64 MiB of HBM per device.

v0:
```python
import math
import jax
import jax.numpy as jnp
from jax import lax
from jax.sharding import PartitionSpec as P

EB = 128
RTILE = 64
norm_eps = 1e-05


def passed_along(array, axis, by):
    count = lax.axis_size(axis)
    return lax.ppermute(array, axis, [(i, (i + by) % count) for i in range(count)])


def layer_norm(pre_act):
    row_mean = jnp.mean(pre_act, axis=-1, keepdims=True)
    centre = pre_act - row_mean
    inv_dev = lax.rsqrt(jnp.mean(centre * centre, axis=-1, keepdims=True) + norm_eps)
    return (centre * inv_dev, inv_dev)


def norm_back(grad_in, normed, inv_dev):
    return inv_dev * (
        grad_in
        - jnp.mean(grad_in, axis=-1, keepdims=True)
        - normed * jnp.mean(grad_in * normed, axis=-1, keepdims=True)
    )


def silu_slope(pre_act):
    sigmoid_v = jax.nn.sigmoid(pre_act)
    return sigmoid_v * (1.0 + pre_act * (1.0 - sigmoid_v))


def dot_left_t(left_op, right_op):
    return lax.dot_general(
        left_op, right_op, (((0,), (0,)), ((), ())), preferred_element_type=jnp.float32
    )


def dot_right_t(left_op, right_op):
    return lax.dot_general(
        left_op, right_op, (((1,), (1,)), ((), ())), preferred_element_type=jnp.float32
    )


def mlp_forward(inputs, w_first, b_first, w_second, b_second):
    pre_act = jnp.dot(inputs, w_first, preferred_element_type=jnp.float32) + b_first
    hidden = jax.nn.silu(pre_act).astype(jnp.bfloat16)
    normed, inv_dev = layer_norm(
        jnp.dot(hidden, w_second, preferred_element_type=jnp.float32) + b_second
    )
    return (pre_act, hidden, normed, inv_dev)


def mlp_back_parts(inputs, w_second, pre_act, hidden, normed, inv_dev, grad_out):
    grad_second = norm_back(grad_out, normed, inv_dev)
    second_b = grad_second.astype(jnp.bfloat16)
    gw_second = dot_left_t(hidden, second_b)
    gb_second = jnp.sum(grad_second, axis=0)
    grad_first = dot_right_t(second_b, w_second) * silu_slope(pre_act)
    first_b = grad_first.astype(jnp.bfloat16)
    gw_first = dot_left_t(inputs, first_b)
    gb_first = jnp.sum(grad_first, axis=0)
    return (first_b, gw_first, gb_first, gw_second, gb_second)


def mlp_backward(inputs, w_first, w_second, pre_act, hidden, normed, inv_dev, grad_out):
    parts = mlp_back_parts(inputs, w_second, pre_act, hidden, normed, inv_dev, grad_out)
    return (dot_right_t(parts[0], w_first),) + parts[1:]


def tile_sum(running, recv_ids, values):
    tile_base = recv_ids[0] // RTILE * RTILE
    local_ids = recv_ids - tile_base
    onehot = local_ids[:, None] == jnp.arange(RTILE, dtype=jnp.int32)[None, :]
    if values.dtype == jnp.bfloat16:
        tile_part = dot_left_t(onehot.astype(jnp.bfloat16), values)
    else:
        tile_part = lax.dot_general(
            onehot.astype(jnp.float32),
            values,
            (((0,), (0,)), ((), ())),
            precision=lax.Precision.HIGHEST,
            preferred_element_type=jnp.float32,
        )
    current = lax.dynamic_slice_in_dim(running, tile_base, RTILE, 0)
    return lax.dynamic_update_slice_in_dim(running, current + tile_part, tile_base, 0)


def on_device(
    node_latent,
    edge_latent,
    grad_out_node,
    grad_out_edge,
    senders,
    receivers,
    band_edges,
    halo_list,
    sea_mask,
    edge_w1,
    edge_b1,
    edge_w2,
    edge_b2,
    node_w1,
    node_b1,
    node_w2,
    node_b2,
):
    features = node_latent.shape[1]
    helpers = lax.axis_size("helper")
    band_count = lax.axis_size("band")
    helper_idx = lax.axis_index("helper")
    band_idx = lax.axis_index("band")
    node_dev = node_latent.shape[0]
    band_size = node_dev * helpers
    halo_size = halo_list.shape[1]
    edge_block = EB
    slot_count = edge_latent.shape[0] // edge_block
    edge_blocks = edge_latent.reshape(slot_count, edge_block, features)
    grad_blocks = grad_out_edge.reshape(slot_count, edge_block, features)
    send_blocks = senders.reshape(slot_count, edge_block)
    recv_blocks = receivers.reshape(slot_count, edge_block)
    halo_ids = halo_list[0]
    band_rows = lax.all_gather(node_latent, "helper", axis=0, tiled=True)
    outgoing = band_rows[halo_ids]
    from_prev = passed_along(outgoing, "band", 1)
    from_next = passed_along(outgoing, "band", -1)
    lookup = jnp.concatenate([band_rows, from_prev, from_next], axis=0)
    live_count = band_edges[band_idx]
    own_live = jnp.clip((live_count - helper_idx + helpers - 1) // helpers, 0, slot_count)

    def inputs_of(slot_id):
        return jnp.concatenate(
            [lookup[send_blocks[slot_id]], band_rows[recv_blocks[slot_id]], edge_blocks[slot_id]],
            axis=1,
        )

    def message_of(inputs):
        normed = mlp_forward(inputs, edge_w1, edge_b1, edge_w2, edge_b2)[2]
        return normed.astype(jnp.bfloat16)

    def add_own(slot_id, agg_rows):
        return tile_sum(agg_rows, recv_blocks[slot_id], message_of(inputs_of(slot_id)))

    agg_start = jnp.zeros((band_size, features), jnp.float32)
    agg_rows = lax.fori_loop(0, own_live, add_own, agg_start)
    agg_own = lax.psum_scatter(agg_rows, "helper", scatter_dimension=0, tiled=True)
    node_in = jnp.concatenate([node_latent, agg_own.astype(jnp.bfloat16)], axis=1)
    n_pre, n_hidden, n_normed, n_inv = mlp_forward(node_in, node_w1, node_b1, node_w2, node_b2)
    node_seed = sea_mask[:, None].astype(jnp.float32) * grad_out_node.astype(jnp.float32)
    node_back = mlp_backward(node_in, node_w1, node_w2, n_pre, n_hidden, n_normed, n_inv, node_seed)
    agg_grad = node_back[0][:, features:].astype(jnp.bfloat16)
    agg_band = lax.all_gather(agg_grad, "helper", axis=0, tiled=True)

    def edge_parts(inputs, grad_edge_in, agg_rows_in):
        msg_grad = grad_edge_in.astype(jnp.float32) + agg_rows_in.astype(jnp.float32)
        pre_act, hidden, normed, inv_dev = mlp_forward(inputs, edge_w1, edge_b1, edge_w2, edge_b2)
        return mlp_back_parts(inputs, edge_w2, pre_act, hidden, normed, inv_dev, msg_grad)

    def settle(lookup_grad, edge_out, slot_id, first_b):
        grad_inputs = dot_right_t(first_b, edge_w1)
        lookup_grad = lookup_grad.at[send_blocks[slot_id]].add(grad_inputs[:, :features])
        lookup_grad = tile_sum(
            lookup_grad, recv_blocks[slot_id], grad_inputs[:, features : 2 * features]
        )
        edge_new = (
            grad_blocks[slot_id].astype(jnp.float32) + grad_inputs[:, 2 * features :]
        ).astype(jnp.bfloat16)
        return (lookup_grad, edge_out.at[slot_id].set(edge_new))

    def own_step(slot_id, loop_state):
        first_b, gw_one, gb_one, gw_two, gb_two = edge_parts(
            inputs_of(slot_id), grad_blocks[slot_id], agg_band[recv_blocks[slot_id]]
        )
        lookup_grad, edge_out = settle(loop_state[0], loop_state[1], slot_id, first_b)
        return (
            lookup_grad,
            edge_out,
            loop_state[2] + gw_one,
            loop_state[3] + gb_one,
            loop_state[4] + gw_two,
            loop_state[5] + gb_two,
        )

    start_state = (
        jnp.zeros((band_size + 2 * halo_size, features), jnp.float32),
        jnp.zeros((slot_count, edge_block, features), jnp.bfloat16),
        jnp.zeros(edge_w1.shape, jnp.float32),
        jnp.zeros((features,), jnp.float32),
        jnp.zeros(edge_w2.shape, jnp.float32),
        jnp.zeros((features,), jnp.float32),
    )
    final_state = lax.fori_loop(0, own_live, own_step, start_state)
    lookup_grad, edge_out = (final_state[0], final_state[1])
    edge_wgrads = final_state[2:]
    band_grad = lookup_grad[:band_size]
    prev_region = lookup_grad[band_size : band_size + halo_size]
    next_region = lookup_grad[band_size + halo_size :]
    from_next_band = passed_along(prev_region.astype(jnp.bfloat16), "band", -1).astype(
        prev_region.dtype
    )
    from_prev_band = passed_along(next_region.astype(jnp.bfloat16), "band", 1).astype(
        next_region.dtype
    )
    band_grad = band_grad.at[halo_ids].add(from_next_band + from_prev_band)
    node_sum = lax.psum_scatter(
        band_grad.astype(jnp.bfloat16), "helper", scatter_dimension=0, tiled=True
    ).astype(jnp.float32)
    grad_node = node_sum + grad_out_node.astype(jnp.float32) + node_back[0][:, :features]
    edge_scale = 1.0 / math.sqrt(slot_count * edge_block * helpers * band_count)
    node_scale = 1.0 / math.sqrt(node_dev * helpers * band_count)
    sums = lax.psum(
        (
            edge_wgrads[0] * edge_scale,
            edge_wgrads[1] * edge_scale,
            edge_wgrads[2] * edge_scale,
            edge_wgrads[3] * edge_scale,
            node_back[1] * node_scale,
            node_back[2] * node_scale,
            node_back[3] * node_scale,
            node_back[4] * node_scale,
        ),
        ("band", "helper"),
    )
    grad_edge = edge_out.reshape(slot_count * edge_block, features)
    return (
        grad_node,
        grad_edge,
        sums[0],
        sums[1],
        sums[2],
        sums[3],
        sums[4],
        sums[5],
        sums[6],
        sums[7],
    )


def solution(mesh):
    in_specs = (
        P(("band", "helper"), None),
        P(("band", "helper"), None),
        P(("band", "helper"), None),
        P(("band", "helper"), None),
        P(("band", "helper")),
        P(("band", "helper")),
        P(),
        P("band", None),
        P(("band", "helper")),
        P(),
        P(),
        P(),
        P(),
        P(),
        P(),
        P(),
        P(),
    )
    out_specs = (
        P(("band", "helper"), None),
        P(("band", "helper"), None),
        P(),
        P(),
        P(),
        P(),
        P(),
        P(),
        P(),
        P(),
    )
    return jax.shard_map(
        on_device, mesh=mesh, in_specs=in_specs, out_specs=out_specs, check_vma=False
    )
```

profile of v0, /device:TPU:0, one launch (start us, length us, event | category | flops | bytes accessed | tf_op | source)
XLA Modules:
  0.0 384.1 jit_solution(12179185624823476819)
XLA Ops:
  7.3 5.9 %all_gather.6 = bf16[128,256]{1,0:T(8,128)(2,1)S(1)} all-gather(bf16[64,256]{1,0:T(8,128)(2,1)} %param.23), channel_id=1, replica_groups=mesh['band'=16,'helper'=2] {'helper'}, dimensions={0}, use_global_device_ids=true | all-gather | bytes 98304 | tf_op jit(solution)/shard_map/all_gather | solution.py:127
  14.5 4.4 %collective-permute-start.1 = (bf16[32,256]{1,0:T(8,128)(2,1)S(1)}, bf16[32,256]{1,0:T(8,128)(2,1)S(1)}, u32[]{:S(2)}, u32[]{:S(2)}) collective-permute-start(bf16[32,256]{1,0:T(8,128)(2,1)S(1)} %gather_fusion.5), channel_id=1, source_target_pairs={{0,30},{2,0},{4,2},{6,4},{8,6},{10,8},{12,10},{14,12},{16,14},{18,... | collective-permute-start | bytes 49160 | tf_op jit(solution)/shard_map/ppermute | solution.py:14
  21.5 11.5 %while.35 = (s32[]{:T(128)}, f32[128,256]{1,0:T(8,128)S(1)}, s32[]{:T(128)}, s32[8,128]{1,0:T(8,128)}, s32[8,128]{1,0:T(8,128)}, /*index=5*/bf16[192,256]{1,0:T(...) while((s32[]{:T(128)}, f32[128,256]{1,0:T(8,128)S(1)}, ...), condition=%wide.region_3.4_spmd, body=%wide.region_0.3_spmd.sunk | while | flops 72379416 | bytes 1659831 | solution.py:149
  25.7 1.1 fusion.120
  31.5 1.1 fusion.120
  34.4 42.2 %reduce-scatter.3.cloned.1.call-done = f32[64,256]{1,0:T(8,128)} async-done(((f32[128,256]{1,0:T(8,128)}), f32[64,256]{1,0:T(8,128)}) %reduce-scatter.3.cloned.1.call-update) | async-done | bytes 65552 | tf_op jit(solution)/shard_map/reduce_scatter | solution.py:150
  81.3 1.0 convolution_multiply_fusion.1
  82.4 4.6 %all_gather.7 = bf16[128,256]{1,0:T(8,128)(2,1)S(1)} all-gather(bf16[64,256]{1,0:T(8,128)(2,1)S(1)} %slice.106), channel_id=1, replica_groups=mesh['band'=16,'helper'=2] {'helper'}, dimensions={0}, use_global_device_ids=true | all-gather | bytes 98304 | tf_op jit(solution)/shard_map/all_gather | solution.py:156
  87.1 32.5 %while.36 = (s32[]{:T(128)}, f32[192,256]{1,0:T(8,128)S(1)}, bf16[8,128,256]{2,1,0:T(8,128)(2,1)S(1)}, f32[768,256]{1,0:T(8,128)S(1)}, f32[256]{0:T(256)S(1)}, /...) while((s32[]{:T(128)}, f32[192,256]{1,0:T(8,128)S(1)}, ...), condition=%wide.region_18.19_spmd, body=%wide.region_9.18_spmd.sunk | while | flops 229600272 | bytes 8176405 | solution.py:196
  93.4 1.0 fusion.135
  94.5 1.0 fusion.136
  96.5 1.5 scatter_custom_fusion.7
  99.9 1.5 fusion.140
  109.6 1.0 fusion.135
  110.6 1.0 fusion.136
  112.7 1.5 scatter_custom_fusion.7
  116.1 1.5 fusion.140
  119.6 14.7 %collective-permute-start.3 = (bf16[32,256]{1,0:T(8,128)(2,1)S(1)}, bf16[32,256]{1,0:T(8,128)(2,1)S(1)}, u32[]{:S(2)}, u32[]{:S(2)}) collective-permute-start(bf16[32,256]{1,0:T(8,128)(2,1)S(1)} %get-tuple-element.515), channel_id=1, source_target_pairs={{0,2},{2,4},{4,6},{6,8},{8,10},{10,12},{12,14},{14,16},{16,18},{18... | collective-permute-start | bytes 49160 | tf_op jit(solution)/shard_map/ppermute | solution.py:14
  134.3 3.9 %collective-permute-start.2 = (bf16[32,256]{1,0:T(8,128)(2,1)S(1)}, bf16[32,256]{1,0:T(8,128)(2,1)S(1)}, u32[]{:S(2)}, u32[]{:S(2)}) collective-permute-start(bf16[32,256]{1,0:T(8,128)(2,1)S(1)} %get-tuple-element.514), channel_id=1, source_target_pairs={{0,30},{2,0},{4,2},{6,4},{8,6},{10,8},{12,10},{14,12},{16,14},{18,... | collective-permute-start | bytes 49160 | tf_op jit(solution)/shard_map/ppermute | solution.py:14
  139.9 79.1 %collective-permute-done.2 = bf16[32,256]{1,0:T(8,128)(2,1)S(1)} collective-permute-done((bf16[32,256]{1,0:T(8,128)(2,1)S(1)}, bf16[32,256]{1,0:T(8,128)(2,1)S(1)}, u32[]{:S(2)}, u32[]{:S(2)}) %collective-permute-start.2) | collective-permute-done | bytes 16416 | tf_op jit(solution)/shard_map/ppermute | solution.py:14
  223.9 41.4 %all-reduce = (f32[256]{0:T(256)}, f32[256]{0:T(256)}, f32[256]{0:T(256)}, f32[256]{0:T(256)}) all-reduce(f32[256]{0:T(256)S(1)} %broadcast_multiply_fusion.9, f32[256]{0:T(256)S(1)} %broadcast_multiply_fusion.8, f32[256]{0:T(256)S(1)} %broadcast_multiply_fusion.7, ...), channel_id=1, replica_groups=mesh['band'=16,'helper'=2] {'band','helper'}, use_global_device_ids=true, to_apply=%region_22.23 | all-reduce | flops 1024 | bytes 8192 | tf_op jit(solution)/shard_map/psum | solution.py:215
  265.3 1.4 fusion.47
  266.7 105.9 %all-reduce.4.cloned.1.call-done = (f32[768,256]{1,0:T(8,128)}, f32[256,256]{1,0:T(8,128)}, f32[512,256]{1,0:T(8,128)}, f32[256,256]{1,0:T(8,128)}) async-done(((f32[768,256]{1,0:T(8,128)}, f32[256,256]{1,0:T(8,128)}, f32[512,256]{1,0:T(8,128)}, f32[256,256]{1,0:T(8,128)}), (f32[768,256]{1,0:T(8,128)}, f32[256,256]{1,0:T(8,128)}, f32[512,256]{1,0:T(8,128)}, ...) | async-done | bytes 1835024 | tf_op jit(solution)/shard_map/psum | solution.py:215
  372.6 2.1 copy.65
  (203 shorter events, 49.3 us)
Async XLA Ops:
  7.2 70.3 %copy-start = (bf16[512,256]{1,0:T(8,128)(2,1)S(1)}, bf16[512,256]{1,0:T(8,128)(2,1)}, u32[]{:S(2)}) copy-start(bf16[512,256]{1,0:T(8,128)(2,1)} %param.36) | copy-start | bytes 786436
  7.2 6.0 %copy-start.30 = (s32[1,32]{1,0:T(1,128)S(1)}, s32[1,32]{1,0:T(1,128)}, u32[]{:S(2)}) copy-start(s32[1,32]{1,0:T(1,128)} %param.30) | copy-start | bytes 388
  7.2 13.7 %copy-start.1 = (bf16[768,256]{1,0:T(8,128)(2,1)S(1)}, bf16[768,256]{1,0:T(8,128)(2,1)}, u32[]{:S(2)}) copy-start(bf16[768,256]{1,0:T(8,128)(2,1)} %param.32) | copy-start | bytes 1179652
  7.2 69.4 %reduce-scatter.3.cloned.1.call-start = ((), (), s32[]{:S(2)}) async-start(), calls=%async_computation.2 | async-start | bytes 196608 | tf_op jit(solution)/shard_map/reduce_scatter | solution.py:150
  14.4 6.4 %collective-permute-start = (bf16[32,256]{1,0:T(8,128)(2,1)S(1)}, bf16[32,256]{1,0:T(8,128)(2,1)S(1)}, u32[]{:S(2)}, u32[]{:S(2)}) collective-permute-start(bf16[32,256]{1,0:T(8,128)(2,1)S(1)} %gather_fusion.5), channel_id=1, source_target_pairs={{0,2},{2,4},{4,6},{6,8},{8,10},{10,12},{12,14},{14,16},{16,18},{18... | collective-permute-start | bytes 49160 | tf_op jit(solution)/shard_map/ppermute | solution.py:14
  14.5 6.4 %collective-permute-start.1 = (bf16[32,256]{1,0:T(8,128)(2,1)S(1)}, bf16[32,256]{1,0:T(8,128)(2,1)S(1)}, u32[]{:S(2)}, u32[]{:S(2)}) collective-permute-start(bf16[32,256]{1,0:T(8,128)(2,1)S(1)} %gather_fusion.5), channel_id=1, source_target_pairs={{0,30},{2,0},{4,2},{6,4},{8,6},{10,8},{12,10},{14,12},{16,14},{18,... | collective-permute-start | bytes 49160 | tf_op jit(solution)/shard_map/ppermute | solution.py:14
  18.9 2.0 copy-start.23
  33.8 231.5 %reduce-scatter.5.cloned.1.call-start = ((), (), s32[]{:S(2)}) async-start(), calls=%async_computation.3 | async-start | bytes 98304 | tf_op jit(solution)/shard_map/reduce_scatter | solution.py:209
  34.4 43.0 %copy-start.7 = (bf16[64,256]{1,0:T(8,128)(2,1)S(1)}, bf16[64,256]{1,0:T(8,128)(2,1)}, u32[]{:S(2)}) copy-start(bf16[64,256]{1,0:T(8,128)(2,1)} %param.23) | copy-start | bytes 98308
  34.4 43.0 %copy-start.19 = (f32[256]{0:T(256)S(1)}, f32[256]{0:T(256)}, u32[]{:S(2)}) copy-start(f32[256]{0:T(256)} %param.37) | copy-start | bytes 3076
  78.4 1.9 copy-start.11
  87.1 4.0 %copy-start.28 = (f32[256]{0:T(256)}, f32[256]{0:T(256)S(1)}, u32[]{:S(2)}) copy-start(f32[256]{0:T(256)S(1)} %get-tuple-element.884) | copy-start | bytes 3076 | tf_op jit(solution)/shard_map/while
  87.1 8.3 %copy-start.24 = (bf16[256,256]{1,0:T(8,128)(2,1)}, bf16[256,256]{1,0:T(8,128)(2,1)S(1)}, u32[]{:S(2)}) copy-start(bf16[256,256]{1,0:T(8,128)(2,1)S(1)} %get-tuple-element.885) | copy-start | bytes 393220 | tf_op jit(solution)/shard_map/while
  87.9 2.4 copy-start.16
  103.4 4.0 %copy-start.28 = (f32[256]{0:T(256)}, f32[256]{0:T(256)S(1)}, u32[]{:S(2)}) copy-start(f32[256]{0:T(256)S(1)} %get-tuple-element.884) | copy-start | bytes 3076 | tf_op jit(solution)/shard_map/while
  103.4 8.3 %copy-start.24 = (bf16[256,256]{1,0:T(8,128)(2,1)}, bf16[256,256]{1,0:T(8,128)(2,1)S(1)}, u32[]{:S(2)}) copy-start(bf16[256,256]{1,0:T(8,128)(2,1)S(1)} %get-tuple-element.885) | copy-start | bytes 393220 | tf_op jit(solution)/shard_map/while
  104.1 2.4 copy-start.16
  119.6 19.6 %copy-start.3 = (bf16[8,128,256]{2,1,0:T(8,128)(2,1)}, bf16[8,128,256]{2,1,0:T(8,128)(2,1)S(1)}, u32[]{:S(2)}) copy-start(bf16[8,128,256]{2,1,0:T(8,128)(2,1)S(1)} %get-tuple-element.419) | copy-start | bytes 1572868
  119.6 20.3 %collective-permute-start.3 = (bf16[32,256]{1,0:T(8,128)(2,1)S(1)}, bf16[32,256]{1,0:T(8,128)(2,1)S(1)}, u32[]{:S(2)}, u32[]{:S(2)}) collective-permute-start(bf16[32,256]{1,0:T(8,128)(2,1)S(1)} %get-tuple-element.515), channel_id=1, source_target_pairs={{0,2},{2,4},{4,6},{6,8},{8,10},{10,12},{12,14},{14,16},{16,18},{18... | collective-permute-start | bytes 49160 | tf_op jit(solution)/shard_map/ppermute | solution.py:14
  134.3 84.7 %collective-permute-start.2 = (bf16[32,256]{1,0:T(8,128)(2,1)S(1)}, bf16[32,256]{1,0:T(8,128)(2,1)S(1)}, u32[]{:S(2)}, u32[]{:S(2)}) collective-permute-start(bf16[32,256]{1,0:T(8,128)(2,1)S(1)} %get-tuple-element.514), channel_id=1, source_target_pairs={{0,30},{2,0},{4,2},{6,4},{8,6},{10,8},{12,10},{14,12},{16,14},{18,... | collective-permute-start | bytes 49160 | tf_op jit(solution)/shard_map/ppermute | solution.py:14
  220.7 151.9 %all-reduce.4.cloned.1.call-start = ((), (), s32[]{:S(2)}) async-start(), calls=%async_computation.4 | async-start | bytes 3670016 | tf_op jit(solution)/shard_map/psum | solution.py:215
  222.4 42.9 %copy-start.6 = (f32[64,512]{1,0:T(8,128)S(1)}, f32[64,512]{1,0:T(8,128)}, u32[]{:S(2)}) copy-start(f32[64,512]{1,0:T(8,128)} %copy-done.5) | copy-start | bytes 393220
  372.6 2.1 copy-start.10
  374.7 1.1 copy-start.4
  (23 other events, 17.6 us)
Sparse Core Ops, SparseCore 0:
  33.9 42.6 reduce-scatter.2
  220.8 10.2 reduce-scatter.4
  238.0 134.4 all-reduce.3
where the time goes:
time: 389 us; the launch traced here: 384 us
  waiting for transfers between devices  227 us (58%)
  blocking collectives  51.9 us (13%)
  local copies, waits for them, and re-layouts  28.9 us (7%)
  other arithmetic  24.6 us (6%)
  starting transfers between devices  23.2 us (6%)
  between operations  14.8 us (4%)
  matrix products  12.4 us (3%)
    psum x1, waiting for transfers between devices, on_device(): lax.psum((edge_wgrads[0] * edge_scale, edge_wgrads[1] * edge_scale, edge_...  106 us
    ppermute x4, waiting for transfers between devices, passed_along(): lax.ppermute(array, axis, [(i, (i + by) % count) for i in range(count)])  79.1 us
    reduce_scatter x1, waiting for transfers between devices, on_device(): lax.psum_scatter(agg_rows, 'helper', scatter_dimension=0, tiled=True)  42.2 us
    psum x1, blocking collectives, on_device(): lax.psum((edge_wgrads[0] * edge_scale, edge_wgrads[1] * edge_scale, edge_...  41.4 us
    ppermute x4, starting transfers between devices, passed_along(): lax.ppermute(array, axis, [(i, (i + by) % count) for i in range(count)])  23.1 us
    unnamed x58, local copies, waits for them, and re-layouts  11.6 us
  transfers between devices with their start and end apart: 7, of which 3 were waited for; matrix products, arithmetic and copies ran while one was open for 1% of the time, Pallas kernels for 0%

commit v1 on v0

--- a/solution.py
+++ b/solution.py
@@ -213,17 +213,20 @@
     edge_scale = 1.0 / math.sqrt(slot_count * edge_block * helpers * band_count)
     node_scale = 1.0 / math.sqrt(node_dev * helpers * band_count)
     sums = lax.psum(
-        (
-            edge_wgrads[0] * edge_scale,
-            edge_wgrads[1] * edge_scale,
-            edge_wgrads[2] * edge_scale,
-            edge_wgrads[3] * edge_scale,
-            node_back[1] * node_scale,
-            node_back[2] * node_scale,
-            node_back[3] * node_scale,
-            node_back[4] * node_scale,
+        lax.psum(
+            (
+                edge_wgrads[0] * edge_scale,
+                edge_wgrads[1] * edge_scale,
+                edge_wgrads[2] * edge_scale,
+                edge_wgrads[3] * edge_scale,
+                node_back[1] * node_scale,
+                node_back[2] * node_scale,
+                node_back[3] * node_scale,
+                node_back[4] * node_scale,
+            ),
+            "helper",
         ),
-        ("band", "helper"),
+        "band",
     )
     grad_edge = edge_out.reshape(slot_count * edge_block, features)
     return (

time: 389 us -> 404 us (1.039)
  waiting for transfers between devices: 227 us -> 247 us
    psum x0 -> x1, waiting for transfers between devices: none -> 73.4 us  [on_device(): lax.psum(lax.psum((edge_wgrads[0] * edge_scale, edge_wgrads[1] * edge_sca...]
    psum x1, waiting for transfers between devices: 106 us -> 50.6 us  [on_device(): lax.psum((edge_wgrads[0] * edge_scale, edge_wgrads[1] * edge_scale, edge_...]
    psum x1, blocking collectives: 41.4 us -> 4.91 us  [on_device(): lax.psum((edge_wgrads[0] * edge_scale, edge_wgrads[1] * edge_scale, edge_...]
    psum x0 -> x1, blocking collectives: none -> 32.7 us  [on_device(): lax.psum(lax.psum((edge_wgrads[0] * edge_scale, edge_wgrads[1] * edge_sca...]
    unnamed x58 -> x50, local copies, waits for them, and re-layouts: 11.6 us -> 10.8 us
  transfers between devices with their start and end apart: 7 -> 8, of which waited for: 3 -> 5; matrix products, arithmetic and copies ran while one was open for 1% -> 1% of each run, Pallas kernels for 0% -> 0%
where the time goes in v1:
time: 404 us; the launch traced here: 400 us
  waiting for transfers between devices  247 us (61%)
  blocking collectives  48.1 us (12%)
  local copies, waits for them, and re-layouts  28.1 us (7%)
  other arithmetic  24.7 us (6%)
  starting transfers between devices  23.3 us (6%)
  between operations  14.8 us (4%)
  matrix products  12.4 us (3%)
    ppermute x4, waiting for transfers between devices, passed_along(): lax.ppermute(array, axis, [(i, (i + by) % count) for i in range(count)])  80.9 us
    psum x1, waiting for transfers between devices, on_device(): lax.psum(lax.psum((edge_wgrads[0] * edge_scale, edge_wgrads[1] * edge_sca...  73.4 us
    psum x1, waiting for transfers between devices, on_device(): lax.psum((edge_wgrads[0] * edge_scale, edge_wgrads[1] * edge_scale, edge_...  50.6 us
    reduce_scatter x1, waiting for transfers between devices, on_device(): lax.psum_scatter(agg_rows, 'helper', scatter_dimension=0, tiled=True)  42.2 us
    psum x1, blocking collectives, on_device(): lax.psum(lax.psum((edge_wgrads[0] * edge_scale, edge_wgrads[1] * edge_sca...  32.7 us
    ppermute x4, starting transfers between devices, passed_along(): lax.ppermute(array, axis, [(i, (i + by) % count) for i in range(count)])  23.1 us
    unnamed x50, local copies, waits for them, and re-layouts  10.8 us
  transfers between devices with their start and end apart: 8, of which 5 were waited for; matrix products, arithmetic and copies ran while one was open for 1% of the time, Pallas kernels for 0%

profile of v1, /device:TPU:0, one launch (start us, length us, event | category | flops | bytes accessed | tf_op | source)
XLA Modules:
  0.0 399.6 jit_solution(13738853863955252192)
XLA Ops:
  7.3 5.9 %all_gather.6 = bf16[128,256]{1,0:T(8,128)(2,1)S(1)} all-gather(bf16[64,256]{1,0:T(8,128)(2,1)} %param.23), channel_id=1, replica_groups=mesh['band'=16,'helper'=2] {'helper'}, dimensions={0}, use_global_device_ids=true | all-gather | bytes 98304 | tf_op jit(solution)/shard_map/all_gather | solution.py:127
  14.4 4.4 %collective-permute-start.1 = (bf16[32,256]{1,0:T(8,128)(2,1)S(1)}, bf16[32,256]{1,0:T(8,128)(2,1)S(1)}, u32[]{:S(2)}, u32[]{:S(2)}) collective-permute-start(bf16[32,256]{1,0:T(8,128)(2,1)S(1)} %gather_fusion.5), channel_id=1, source_target_pairs={{0,30},{2,0},{4,2},{6,4},{8,6},{10,8},{12,10},{14,12},{16,14},{18,... | collective-permute-start | bytes 49160 | tf_op jit(solution)/shard_map/ppermute | solution.py:14
  21.5 11.5 %while.35 = (s32[]{:T(128)}, f32[128,256]{1,0:T(8,128)S(1)}, s32[]{:T(128)}, s32[8,128]{1,0:T(8,128)}, s32[8,128]{1,0:T(8,128)}, /*index=5*/bf16[192,256]{1,0:T(...) while((s32[]{:T(128)}, f32[128,256]{1,0:T(8,128)S(1)}, ...), condition=%wide.region_3.4_spmd, body=%wide.region_0.3_spmd.sunk | while | flops 72379416 | bytes 1659831 | solution.py:149
  25.6 1.1 fusion.120
  31.4 1.1 fusion.120
  34.4 42.2 %reduce-scatter.3.cloned.1.call-done = f32[64,256]{1,0:T(8,128)} async-done(((f32[128,256]{1,0:T(8,128)}), f32[64,256]{1,0:T(8,128)}) %reduce-scatter.3.cloned.1.call-update) | async-done | bytes 65552 | tf_op jit(solution)/shard_map/reduce_scatter | solution.py:150
  81.2 1.0 convolution_multiply_fusion.1
  83.2 4.6 %all_gather.7 = bf16[128,256]{1,0:T(8,128)(2,1)S(1)} all-gather(bf16[64,256]{1,0:T(8,128)(2,1)S(1)} %slice.106), channel_id=1, replica_groups=mesh['band'=16,'helper'=2] {'helper'}, dimensions={0}, use_global_device_ids=true | all-gather | bytes 98304 | tf_op jit(solution)/shard_map/all_gather | solution.py:156
  88.0 32.5 %while.36 = (s32[]{:T(128)}, f32[192,256]{1,0:T(8,128)S(1)}, bf16[8,128,256]{2,1,0:T(8,128)(2,1)S(1)}, f32[768,256]{1,0:T(8,128)S(1)}, f32[256]{0:T(256)S(1)}, /...) while((s32[]{:T(128)}, f32[192,256]{1,0:T(8,128)S(1)}, ...), condition=%wide.region_18.19_spmd, body=%wide.region_9.18_spmd.sunk | while | flops 229600272 | bytes 8176405 | solution.py:196
  94.3 1.0 fusion.135
  97.4 1.5 scatter_custom_fusion.7
  100.8 1.5 fusion.140
  113.6 1.5 scatter_custom_fusion.7
  117.0 1.5 fusion.140
  122.3 14.7 %collective-permute-start.3 = (bf16[32,256]{1,0:T(8,128)(2,1)S(1)}, bf16[32,256]{1,0:T(8,128)(2,1)S(1)}, u32[]{:S(2)}, u32[]{:S(2)}) collective-permute-start(bf16[32,256]{1,0:T(8,128)(2,1)S(1)} %get-tuple-element.523), channel_id=1, source_target_pairs={{0,2},{2,4},{4,6},{6,8},{8,10},{10,12},{12,14},{14,16},{16,18},{18... | collective-permute-start | bytes 49160 | tf_op jit(solution)/shard_map/ppermute | solution.py:14
  137.0 3.9 collective-permute-start.2
  141.0 1.3 collective-permute-done.3
  142.3 79.5 %collective-permute-done.2 = bf16[32,256]{1,0:T(8,128)(2,1)S(1)} collective-permute-done((bf16[32,256]{1,0:T(8,128)(2,1)S(1)}, bf16[32,256]{1,0:T(8,128)(2,1)S(1)}, u32[]{:S(2)}, u32[]{:S(2)}) %collective-permute-start.2) | collective-permute-done | bytes 16416 | tf_op jit(solution)/shard_map/ppermute | solution.py:14
  223.6 50.6 %all-reduce.9.cloned.1.call-done = (f32[768,256]{1,0:T(8,128)}, f32[256,256]{1,0:T(8,128)}, f32[512,256]{1,0:T(8,128)}, f32[256,256]{1,0:T(8,128)}) async-done(((f32[768,256]{1,0:T(8,128)}, f32[256,256]{1,0:T(8,128)}, f32[512,256]{1,0:T(8,128)}, f32[256,256]{1,0:T(8,128)}), (f32[768,256]{1,0:T(8,128)}, f32[256,256]{1,0:T(8,128)}, f32[512,256]{1,0:T(8,128)}, ...) | async-done | bytes 1835024 | tf_op jit(solution)/shard_map/psum | solution.py:216
  275.6 4.9 %all-reduce.2 = (f32[256]{0:T(256)S(1)}, f32[256]{0:T(256)S(1)}, f32[256]{0:T(256)S(1)}, f32[256]{0:T(256)S(1)}) all-reduce(f32[256]{0:T(256)S(1)} %broadcast_multiply_fusion.9, f32[256]{0:T(256)S(1)} %broadcast_multiply_fusion.8, f32[256]{0:T(256)S(1)} %broadcast_multiply_fusion.7, ...), channel_id=1, replica_groups=mesh['band'=16,'helper'=2] {'helper'}, use_global_device_ids=true, to_apply=%region_23.24 | all-reduce | flops 1024 | bytes 8192 | tf_op jit(solution)/shard_map/psum | solution.py:216
  280.5 32.7 %all-reduce = (f32[256]{0:T(256)}, f32[256]{0:T(256)}, f32[256]{0:T(256)}, f32[256]{0:T(256)}) all-reduce(f32[256]{0:T(256)S(1)} %get-tuple-element.498, f32[256]{0:T(256)S(1)} %get-tuple-element.499, f32[256]{0:T(256)S(1)} %get-tuple-element.500, f32[256]{0:T(256)S(1)} %get-tuple-element.501), channel_id=1, replica_groups=mesh['band'=16,'helper'=2] {'band'}, use_global_device_ids=true, to_apply=%region_24.25 | all-reduce | flops 1024 | bytes 8192 | tf_op jit(solution)/shard_map/psum | solution.py:215
  313.2 1.4 fusion.47
  314.6 73.4 %all-reduce.7.cloned.1.call-done = (f32[768,256]{1,0:T(8,128)}, f32[256,256]{1,0:T(8,128)}, f32[512,256]{1,0:T(8,128)}, f32[256,256]{1,0:T(8,128)}) async-done(((f32[768,256]{1,0:T(8,128)}, f32[256,256]{1,0:T(8,128)}, f32[512,256]{1,0:T(8,128)}, f32[256,256]{1,0:T(8,128)}), (f32[768,256]{1,0:T(8,128)}, f32[256,256]{1,0:T(8,128)}, f32[512,256]{1,0:T(8,128)}, ...) | async-done | bytes 1835024 | tf_op jit(solution)/shard_map/psum | solution.py:215
  388.0 2.1 copy.69
  (199 shorter events, 51.7 us)
Async XLA Ops:
  7.2 70.2 %copy-start = (bf16[512,256]{1,0:T(8,128)(2,1)S(1)}, bf16[512,256]{1,0:T(8,128)(2,1)}, u32[]{:S(2)}) copy-start(bf16[512,256]{1,0:T(8,128)(2,1)} %param.36) | copy-start | bytes 786436
  7.2 6.0 %copy-start.26 = (s32[1,32]{1,0:T(1,128)S(1)}, s32[1,32]{1,0:T(1,128)}, u32[]{:S(2)}) copy-start(s32[1,32]{1,0:T(1,128)} %param.30) | copy-start | bytes 388
  7.2 13.6 %copy-start.1 = (bf16[768,256]{1,0:T(8,128)(2,1)S(1)}, bf16[768,256]{1,0:T(8,128)(2,1)}, u32[]{:S(2)}) copy-start(bf16[768,256]{1,0:T(8,128)(2,1)} %param.32) | copy-start | bytes 1179652
  7.2 69.3 %reduce-scatter.3.cloned.1.call-start = ((), (), s32[]{:S(2)}) async-start(), calls=%async_computation.2 | async-start | bytes 196608 | tf_op jit(solution)/shard_map/reduce_scatter | solution.py:150
  14.3 6.4 %collective-permute-start = (bf16[32,256]{1,0:T(8,128)(2,1)S(1)}, bf16[32,256]{1,0:T(8,128)(2,1)S(1)}, u32[]{:S(2)}, u32[]{:S(2)}) collective-permute-start(bf16[32,256]{1,0:T(8,128)(2,1)S(1)} %gather_fusion.5), channel_id=1, source_target_pairs={{0,2},{2,4},{4,6},{6,8},{8,10},{10,12},{12,14},{14,16},{16,18},{18... | collective-permute-start | bytes 49160 | tf_op jit(solution)/shard_map/ppermute | solution.py:14
  14.4 6.4 %collective-permute-start.1 = (bf16[32,256]{1,0:T(8,128)(2,1)S(1)}, bf16[32,256]{1,0:T(8,128)(2,1)S(1)}, u32[]{:S(2)}, u32[]{:S(2)}) collective-permute-start(bf16[32,256]{1,0:T(8,128)(2,1)S(1)} %gather_fusion.5), channel_id=1, source_target_pairs={{0,30},{2,0},{4,2},{6,4},{8,6},{10,8},{12,10},{14,12},{16,14},{18,... | collective-permute-start | bytes 49160 | tf_op jit(solution)/shard_map/ppermute | solution.py:14
  18.8 2.0 copy-start.19
  33.7 240.5 %all-reduce.9.cloned.1.call-start = ((), (), s32[]{:S(2)}) async-start(), calls=%async_computation.5 | async-start | bytes 3670016 | tf_op jit(solution)/shard_map/psum | solution.py:216
  34.4 43.0 %copy-start.7 = (bf16[64,256]{1,0:T(8,128)(2,1)S(1)}, bf16[64,256]{1,0:T(8,128)(2,1)}, u32[]{:S(2)}) copy-start(bf16[64,256]{1,0:T(8,128)(2,1)} %param.23) | copy-start | bytes 98308
  34.4 43.0 %copy-start.15 = (f32[256]{0:T(256)S(1)}, f32[256]{0:T(256)}, u32[]{:S(2)}) copy-start(f32[256]{0:T(256)} %param.37) | copy-start | bytes 3076
  81.2 2.0 copy-start.5
  88.0 4.0 %copy-start.24 = (f32[256]{0:T(256)}, f32[256]{0:T(256)S(1)}, u32[]{:S(2)}) copy-start(f32[256]{0:T(256)S(1)} %get-tuple-element.892) | copy-start | bytes 3076 | tf_op jit(solution)/shard_map/while
  88.0 8.3 %copy-start.20 = (bf16[256,256]{1,0:T(8,128)(2,1)}, bf16[256,256]{1,0:T(8,128)(2,1)S(1)}, u32[]{:S(2)}) copy-start(bf16[256,256]{1,0:T(8,128)(2,1)S(1)} %get-tuple-element.893) | copy-start | bytes 393220 | tf_op jit(solution)/shard_map/while
  88.8 2.4 copy-start.12
  104.3 4.0 copy-start.24
  104.3 8.3 %copy-start.20 = (bf16[256,256]{1,0:T(8,128)(2,1)}, bf16[256,256]{1,0:T(8,128)(2,1)S(1)}, u32[]{:S(2)}) copy-start(bf16[256,256]{1,0:T(8,128)(2,1)S(1)} %get-tuple-element.893) | copy-start | bytes 393220 | tf_op jit(solution)/shard_map/while
  105.0 2.4 copy-start.12
  122.3 190.9 %reduce-scatter.5.cloned.1.call-start = ((), (), s32[]{:S(2)}) async-start(), calls=%async_computation.3 | async-start | bytes 98304 | tf_op jit(solution)/shard_map/reduce_scatter | solution.py:209
  122.3 20.0 %collective-permute-start.3 = (bf16[32,256]{1,0:T(8,128)(2,1)S(1)}, bf16[32,256]{1,0:T(8,128)(2,1)S(1)}, u32[]{:S(2)}, u32[]{:S(2)}) collective-permute-start(bf16[32,256]{1,0:T(8,128)(2,1)S(1)} %get-tuple-element.523), channel_id=1, source_target_pairs={{0,2},{2,4},{4,6},{6,8},{8,10},{10,12},{12,14},{14,16},{16,18},{18... | collective-permute-start | bytes 49160 | tf_op jit(solution)/shard_map/ppermute | solution.py:14
  137.0 84.8 %collective-permute-start.2 = (bf16[32,256]{1,0:T(8,128)(2,1)S(1)}, bf16[32,256]{1,0:T(8,128)(2,1)S(1)}, u32[]{:S(2)}, u32[]{:S(2)}) collective-permute-start(bf16[32,256]{1,0:T(8,128)(2,1)S(1)} %get-tuple-element.522), channel_id=1, source_target_pairs={{0,30},{2,0},{4,2},{6,4},{8,6},{10,8},{12,10},{14,12},{16,14},{18,... | collective-permute-start | bytes 49160 | tf_op jit(solution)/shard_map/ppermute | solution.py:14
  223.5 164.5 %all-reduce.7.cloned.1.call-start = ((), (), s32[]{:S(2)}) async-start(), calls=%async_computation.4 | async-start | bytes 3670016 | tf_op jit(solution)/shard_map/psum | solution.py:215
  274.2 39.0 %copy-start.6 = (f32[64,512]{1,0:T(8,128)S(1)}, f32[64,512]{1,0:T(8,128)}, u32[]{:S(2)}) copy-start(f32[64,512]{1,0:T(8,128)} %copy-done.5) | copy-start | bytes 393220
  388.0 2.1 copy-start.10
  390.1 1.1 copy-start.4
  (20 other events, 15.2 us)
Sparse Core Ops, SparseCore 0:
  33.8 42.6 reduce-scatter.2
  122.4 151.7 all-reduce.8
  276.9 10.0 reduce-scatter.4
  290.7 97.2 all-reduce.6
